TPU v7x, 128 devices: a whole 4x4x4 slice. The times are simulated.
128 devices in a mesh: dp: 8 (over y, core), feat: 16 (over z, x).
Axes of the slice: x: 4, y: 4, z: 4, core: 2. Of those that a mesh axis runs over, the one named last changes fastest.
Arguments:
- features: bfloat16 [32768, 8192], P('dp', 'feat'), may hold values from -6 to 6
- fixed_coef: float32 [8192], P('feat'), may hold values from -0.0625 to 0.0625
- member_score: float32 [32768], P('dp'), may hold values from -6 to 6
- clicks: int32 [32768], P('dp'), may hold values 0 or 1
- member_features: bfloat16 [32768, 256], P(('dp', 'feat')), may hold values from -6 to 6
- member_coef: float32 [1024, 256], P(('dp', 'feat')), may hold values from -0.375 to 0.375
- block_slot: int32 [32768], P(('dp', 'feat')), may hold values from 0 to 65535, as said below
Outputs:
- fixed_grad: float32 [8192], P('feat')
- member_coef_new: float32 [1024, 256], P(('dp', 'feat'))
- total_score: float32 [32768], P(('dp', 'feat'))
Inputs may be any that keep to these rules, and one draw needn't show every extreme that they name: All block_slot values differ. block_slot // 512 is the device (index along dp+feat) that owns the impression's member, and block_slot // 64 is the member. Every owner receives exactly 256 impressions. One device sends at most 6 of its impressions to one owner, and every device sends exactly 6 to some owner.
All inputs are finite; a program needn't handle non-finite values. Where the computation divides by a largest or mean magnitude, that divisor is 1e-20 or more. No bound on the sum of `clicks` on one device may be relied on, other than what follows from the above.
Results may differ from a plain program's by a relative error of at most 0.0093.
Values may be sent and summed in bfloat16 or wider, within the bound.
A program may use at most 64 MiB of HBM per device.

v0:
```python
import math
import jax
import jax.numpy as jnp
from jax import lax
from jax.sharding import PartitionSpec as P

BLK = 64
NEWTON = 3
ridge_weight = 1.0
high = lax.Precision.HIGHEST
inverse_sweeps = 20


def apply_inverse(system, vector):
    identity = jnp.eye(system.shape[1], dtype=system.dtype)
    bound = jnp.max(jnp.sum(jnp.abs(system), axis=2), axis=1)
    start = (2.0 / (1.0 + bound))[:, None, None] * identity[None, :, :]

    def sweep(index, approx):
        product = jnp.einsum("mbc,mcd->mbd", system, approx, precision=high)
        return 2.0 * approx - jnp.einsum("mbc,mcd->mbd", approx, product, precision=high)

    approx = lax.fori_loop(0, inverse_sweeps, sweep, start)
    return jnp.einsum("mbc,mc->mb", approx, vector, precision=high)


def newton_blocks(padded_rows, offset, label_pad, live_pad, coeffs):
    gram_matrix = jnp.einsum("mbk,mck->mbc", padded_rows, padded_rows, precision=high)
    identity = jnp.eye(padded_rows.shape[1], dtype=padded_rows.dtype)
    for iteration in range(NEWTON):
        linear = offset + jnp.einsum("mbk,mk->mb", padded_rows, coeffs, precision=high)
        probability = jax.nn.sigmoid(linear)
        gradient = (
            jnp.einsum(
                "mbk,mb->mk", padded_rows, live_pad * (probability - label_pad), precision=high
            )
            + ridge_weight * coeffs
        )
        weight_root = jnp.sqrt(live_pad * probability * (1.0 - probability))
        system = (
            ridge_weight * identity
            + weight_root[:, :, None] * gram_matrix * weight_root[:, None, :]
        )
        projected = weight_root * jnp.einsum("mbk,mk->mb", padded_rows, gradient, precision=high)
        solved = apply_inverse(system, projected)
        back_term = jnp.einsum("mbk,mb->mk", padded_rows, weight_root * solved, precision=high)
        coeffs = coeffs - (gradient - back_term) / ridge_weight
    return coeffs


def per_device(
    features, fixed_coef, member_score, clicks, member_features, member_coef, block_slot
):
    n_dp = lax.axis_size("dp")
    n_feat = lax.axis_size("feat")
    devices = n_dp * n_feat
    rows_own = member_features.shape[0]
    width = member_features.shape[1]
    slot_count = 2 * rows_own
    blocks = slot_count // BLK
    capacity = 3 * ((rows_own + devices - 1) // devices)
    row_start = lax.axis_index("feat") * rows_own
    coef_half = fixed_coef.astype(jnp.bfloat16)
    partial_score = jnp.dot(features, coef_half, preferred_element_type=jnp.float32)
    own_clicks = lax.dynamic_slice_in_dim(clicks, row_start, rows_own).astype(jnp.float32)
    fixed_score = lax.psum(partial_score, "feat")
    residual = (jax.nn.sigmoid(fixed_score + member_score) - clicks.astype(jnp.float32)).astype(
        jnp.bfloat16
    )
    own_score = lax.dynamic_slice_in_dim(fixed_score, row_start, rows_own)
    grad_part = jnp.dot(residual, features, preferred_element_type=jnp.float32)
    fixed_grad = lax.psum(grad_part, "dp") / math.sqrt(rows_own * devices)
    owner_dev = block_slot // slot_count
    local_slot = block_slot - owner_dev * slot_count
    onehot = (owner_dev[:, None] == jnp.arange(devices, dtype=jnp.int32)[None, :]).astype(jnp.int32)
    row_rank = jnp.sum(jnp.cumsum(onehot, axis=0) * onehot, axis=1) - 1
    send_place = owner_dev * capacity + row_rank
    rows_out = (
        jnp.zeros((devices * capacity, width), jnp.bfloat16).at[send_place].set(member_features)
    )
    tag_value = (local_slot * 2).astype(jnp.float32) + own_clicks
    score_buffer = jnp.zeros((devices * capacity,), jnp.float32).at[send_place].set(own_score)
    tag_buffer = jnp.full((devices * capacity,), -1.0, jnp.float32).at[send_place].set(tag_value)
    meta_out = jnp.stack([score_buffer, tag_buffer])
    rows_in = lax.all_to_all(
        rows_out.reshape(devices, capacity, width),
        ("dp", "feat"),
        split_axis=0,
        concat_axis=0,
        tiled=True,
    )
    meta_in = lax.all_to_all(
        meta_out.reshape(2, devices, capacity),
        ("dp", "feat"),
        split_axis=1,
        concat_axis=1,
        tiled=True,
    )
    rows_in = rows_in.reshape(devices * capacity, width)
    meta_in = meta_in.reshape(2, devices * capacity)
    tags_in = meta_in[1]
    valid_slot = tags_in >= 0.0
    tag_int = jnp.where(valid_slot, tags_in, 0.0).astype(jnp.int32)
    label_in = (tag_int % 2).astype(jnp.float32)
    where_local = jnp.where(valid_slot, tag_int // 2, slot_count)
    padded_rows = (
        jnp.zeros((slot_count + 1, width), jnp.float32)
        .at[where_local]
        .set(rows_in.astype(jnp.float32))[:slot_count]
        .reshape(blocks, BLK, width)
    )
    offset = (
        jnp.zeros((slot_count + 1,), jnp.float32)
        .at[where_local]
        .set(meta_in[0])[:slot_count]
        .reshape(blocks, BLK)
    )
    label_pad = (
        jnp.zeros((slot_count + 1,), jnp.float32)
        .at[where_local]
        .set(label_in)[:slot_count]
        .reshape(blocks, BLK)
    )
    live_pad = (
        jnp.zeros((slot_count + 1,), jnp.float32)
        .at[where_local]
        .set(1.0)[:slot_count]
        .reshape(blocks, BLK)
    )
    coeffs = newton_blocks(padded_rows, offset, label_pad, live_pad, member_coef)
    member_value = jnp.einsum("mbk,mk->mb", padded_rows, coeffs, precision=high).reshape(slot_count)
    back_value = jnp.where(valid_slot, member_value[jnp.minimum(where_local, slot_count - 1)], 0.0)
    returned = lax.all_to_all(
        back_value.reshape(devices, capacity),
        ("dp", "feat"),
        split_axis=0,
        concat_axis=0,
        tiled=True,
    )
    returned = returned.reshape(devices * capacity)
    total_score = own_score + returned[send_place]
    return (fixed_grad, coeffs, total_score)


def solution(mesh):
    return jax.shard_map(
        per_device,
        mesh=mesh,
        in_specs=(
            P("dp", "feat"),
            P("feat"),
            P("dp"),
            P("dp"),
            P(("dp", "feat"), None),
            P(("dp", "feat"), None),
            P(("dp", "feat")),
        ),
        out_specs=(P("feat"), P(("dp", "feat"), None), P(("dp", "feat"))),
        check_vma=False,
    )
```

profile of v0, /device:TPU:1, one launch (start us, length us, event | category | flops | bytes accessed | tf_op | source)
XLA Modules:
  0.0 235.6 jit_solution(464150204069671483)
XLA Ops:
  0.7 0.8 convert_add_fusion
  2.1 0.7 convert_element_type.65
  2.8 3.4 %fusion.54 = f32[1,4096]{1,0:T(1,128)S(1)} fusion(bf16[4096,512]{1,0:T(8,128)(2,1)} %param.13, bf16[512,1]{0,1:T(2,128)(2,1)S(1)} %reshape.293), kind=kOutput, calls=%fused_computation.124 | convolution fusion | flops 4194304 | bytes 4211712 | tf_op jit(solution)/shard_map/dot_general | solution.py:64
  6.1 62.3 %psum.14 = f32[4096]{0:T(1024)S(1)} all-reduce(f32[4096]{0:T(1024)S(1)} %bitcast.212), channel_id=1, replica_groups=mesh['dp'=8,'feat'=16] {'feat'}, use_global_device_ids=true, to_apply=%region_0.0 | all-reduce | flops 4096 | bytes 32768 | tf_op jit(solution)/shard_map/psum | solution.py:66
  68.5 1.4 scatter_custom_fusion
  70.0 1.4 scatter_custom_fusion.1
  71.6 0.8 copy.54
  72.3 18.9 %all-to-all-start = ((f32[2,128,6]{2,0,1:T(2,128)}), f32[2,128,6]{2,0,1:T(2,128)S(1)}, u32[]{:S(2)}, u32[]{:S(2)}) async-start(f32[2,128,6]{2,0,1:T(2,128)} %copy.54), calls=%async_computation | async-start | bytes 262144 | tf_op jit(solution)/shard_map/all_to_all | solution.py:92
  91.3 2.8 %fusion.55 = f32[1,512]{1,0:T(1,128)S(1)} fusion(bf16[4096,1]{0,1:T(2,128)(2,1)S(1)} %reshape.295, bf16[4096,512]{1,0:T(8,128)(2,1)} %param.13), kind=kOutput, calls=%fused_computation.125 | convolution fusion | flops 4194304 | bytes 4204544 | tf_op jit(solution)/shard_map/dot_general | solution.py:71
  94.2 12.8 %psum.15 = f32[512]{0:T(512)S(1)} all-reduce(f32[512]{0:T(512)S(1)} %bitcast.239), channel_id=1, replica_groups=mesh['dp'=8,'feat'=16] {'dp'}, use_global_device_ids=true, to_apply=%region_1.0 | all-reduce | flops 512 | bytes 4096 | tf_op jit(solution)/shard_map/psum | solution.py:72
  107.0 0.6 broadcast_multiply_fusion.3
  107.6 2.0 scatter_custom_fusion.2
  109.6 0.9 reshape.209
  110.5 9.4 %all-to-all-start.1 = ((bf16[128,6,256]{2,1,0:T(8,128)(2,1)}), bf16[128,6,256]{2,1,0:T(8,128)(2,1)S(1)}, u32[]{:S(2)}, u32[]{:S(2)}) async-start(bf16[128,6,256]{2,1,0:T(8,128)(2,1)} %reshape.209), calls=%async_computation.1 | async-start | bytes 1048576 | tf_op jit(solution)/shard_map/all_to_all | solution.py:85
  120.5 3.4 %scatter_custom_fusion.6 = f32[513]{0:T(1024)S(1)} fusion(s32[768]{0:T(1024)S(1)} %get-tuple-element.94, f32[768]{0:T(1024)S(1)} %fusion.33, f32[]{:T(128)} %constant.51.clone.1), kind=kCustom, calls=%fused_computation.98 | custom fusion | bytes 2056 | tf_op jit(solution)/shard_map/scatter | solution.py:121
  124.1 3.4 %scatter_custom_fusion.5 = f32[513]{0:T(1024)S(1)} fusion(s32[768]{0:T(1024)S(1)} %get-tuple-element.94, f32[768]{0:T(1024)S(1)} %reshape.277, f32[]{:T(128)} %constant.51.clone.1), kind=kCustom, calls=%fused_computation.100 | custom fusion | bytes 2056 | tf_op jit(solution)/shard_map/scatter | solution.py:115
  127.6 3.6 %scatter_custom_fusion.4 = f32[513]{0:T(1024)S(1)} fusion(s32[768]{0:T(1024)S(1)} %get-tuple-element.94, f32[768]{0:T(1024)S(1)} %broadcast.285, f32[]{:T(128)} %constant.51.clone.1), kind=kCustom, calls=%fused_computation.102 | custom fusion | bytes 2056 | tf_op jit(solution)/shard_map/scatter | solution.py:127
  131.2 2.8 %all-to-all-done.1 = bf16[128,6,256]{2,1,0:T(8,128)(2,1)S(1)} async-done(((bf16[128,6,256]{2,1,0:T(8,128)(2,1)}), bf16[128,6,256]{2,1,0:T(8,128)(2,1)S(1)}, u32[]{:S(2)}, u32[]{:S(2)}) %all-to-all-start.1) | async-done | bytes 393248 | tf_op jit(solution)/shard_map/all_to_all | solution.py:85
  134.1 5.6 %scatter_custom_fusion.3 = f32[513,256]{1,0:T(8,128)S(1)} fusion(s32[768]{0:T(1024)S(1)} %get-tuple-element.94, f32[768,256]{1,0:T(8,128)S(1)} %reshape.261, f32[]{:T(128)} %constant.51.clone.1), kind=kCustom, calls=%fused_computation.15 | custom fusion | bytes 525316 | tf_op jit(solution)/shard_map/scatter | solution.py:109
  139.8 0.6 fusion.27
  141.4 0.6 abs_reduce_fusion.2
  142.4 20.0 %while.30 = (s32[]{:T(128)}, f32[8,64,64]{1,2,0:T(8,128)S(1)}, f32[8,64,64]{2,1,0:T(8,128)S(1)}, s32[]{:T(128)}) while((s32[]{:T(128)}, f32[8,64,64]{1,2,0:T(8,128)S(1)}, f32[8,64,64]{2,1,0:T(8,128)S(1)}, s32[]{:T(128)}) %tuple.70), condition=%wide.region_15.16_spmd, body=%wide.region_14.15_spmd.sunk | while | flops 50397184 | bytes 1048629 | solution.py:23
  163.1 0.6 fusion.23
  165.2 20.0 %while.31 = (s32[]{:T(128)}, f32[8,64,64]{1,2,0:T(8,128)S(1)}, f32[8,64,64]{2,1,0:T(8,128)S(1)}, s32[]{:T(128)}) while((s32[]{:T(128)}, f32[8,64,64]{1,2,0:T(8,128)S(1)}, f32[8,64,64]{2,1,0:T(8,128)S(1)}, s32[]{:T(128)}) %tuple.73), condition=%wide.region_19.20_spmd, body=%wide.region_18.19_spmd.sunk | while | flops 50397184 | bytes 1048629 | solution.py:23
  188.1 20.0 %while.32 = (s32[]{:T(128)}, f32[8,64,64]{1,2,0:T(8,128)S(1)}, f32[8,64,64]{2,1,0:T(8,128)S(1)}, s32[]{:T(128)}) while((s32[]{:T(128)}, f32[8,64,64]{1,2,0:T(8,128)S(1)}, f32[8,64,64]{2,1,0:T(8,128)S(1)}, s32[]{:T(128)}) %tuple.76), condition=%wide.region_23.24_spmd, body=%wide.region_22.23_spmd.sunk | while | flops 50397184 | bytes 1048629 | solution.py:23
  209.5 5.0 %gather_fusion = f32[768]{0:T(1024)S(1)} fusion(f32[512]{0:T(512)S(1)} %reshape.214, s32[1024]{0:T(1024)S(1)} %pad_clamp_fusion.1), kind=kCustom, calls=%fused_computation | custom fusion | bytes 9216 | tf_op jit(solution)/shard_map/gather | solution.py:132
  214.7 0.6 bitcast_select_fusion.1
  215.3 7.0 %all-to-all-start.2 = ((f32[128,1,6]{2,1,0:T(1,128)}), f32[128,1,6]{2,1,0:T(1,128)S(1)}, u32[]{:S(2)}, u32[]{:S(2)}) async-start(f32[128,1,6]{2,1,0:T(1,128)} %bitcast.62), calls=%async_computation.2 | async-start | bytes 131072 | tf_op jit(solution)/shard_map/all_to_all | solution.py:133
  222.3 9.8 %all-to-all-done.2 = f32[128,1,6]{2,1,0:T(1,128)S(1)} async-done(((f32[128,1,6]{2,1,0:T(1,128)}), f32[128,1,6]{2,1,0:T(1,128)S(1)}, u32[]{:S(2)}, u32[]{:S(2)}) %all-to-all-start.2) | async-done | bytes 3104 | tf_op jit(solution)/shard_map/all_to_all | solution.py:133
  232.6 0.8 reduce.11
  233.6 1.4 gather_fusion.1
  234.9 0.6 dynamic-slice_add_fusion
  (271 shorter events, 68.3 us)
Async XLA Ops:
  0.6 90.6 %copy-start.2 = (s32[4096]{0:T(1024)S(1)}, s32[4096]{0:T(1024)}, u32[]{:S(2)}) copy-start(s32[4096]{0:T(1024)} %param.16) | copy-start | bytes 49156
  0.6 90.6 %copy-start.3 = (f32[4096]{0:T(1024)S(1)}, f32[4096]{0:T(1024)}, u32[]{:S(2)}) copy-start(f32[4096]{0:T(1024)} %param.15) | copy-start | bytes 49156
  72.3 38.2 %all-to-all-start = ((f32[2,128,6]{2,0,1:T(2,128)}), f32[2,128,6]{2,0,1:T(2,128)S(1)}, u32[]{:S(2)}, u32[]{:S(2)}) async-start(f32[2,128,6]{2,0,1:T(2,128)} %copy.54), calls=%async_computation | async-start | bytes 262144 | tf_op jit(solution)/shard_map/all_to_all | solution.py:92
  91.3 48.4 %copy-start = (f32[8,256]{1,0:T(8,128)S(1)}, f32[8,256]{1,0:T(8,128)}, u32[]{:S(2)}) copy-start(f32[8,256]{1,0:T(8,128)} %param.18) | copy-start | bytes 24580
  110.5 23.5 %all-to-all-start.1 = ((bf16[128,6,256]{2,1,0:T(8,128)(2,1)}), bf16[128,6,256]{2,1,0:T(8,128)(2,1)S(1)}, u32[]{:S(2)}, u32[]{:S(2)}) async-start(bf16[128,6,256]{2,1,0:T(8,128)(2,1)} %reshape.209), calls=%async_computation.1 | async-start | bytes 1048576 | tf_op jit(solution)/shard_map/all_to_all | solution.py:85
  208.9 26.7 %copy-start.1 = (f32[8,256]{1,0:T(8,128)}, f32[8,256]{1,0:T(8,128)S(1)}, u32[]{:S(2)}) copy-start(f32[8,256]{1,0:T(8,128)S(1)} %fusion.12) | copy-start | bytes 24580
  215.3 16.8 %all-to-all-start.2 = ((f32[128,1,6]{2,1,0:T(1,128)}), f32[128,1,6]{2,1,0:T(1,128)S(1)}, u32[]{:S(2)}, u32[]{:S(2)}) async-start(f32[128,1,6]{2,1,0:T(1,128)} %bitcast.62), calls=%async_computation.2 | async-start | bytes 131072 | tf_op jit(solution)/shard_map/all_to_all | solution.py:133
where the time goes:
time: 236 us
  blocking collectives  75.1 us (32%)
  matrix products  70.7 us (30%)
  starting transfers between devices  35.3 us (15%)
  local copies, waits for them, and re-layouts  32.6 us (14%)
  waiting for transfers between devices  12.6 us (5%)
  other arithmetic  5.86 us (2%)
    psum x1, blocking collectives, per_device(): fixed_score = lax.psum(partial_score, 'feat')  62.3 us
    dot_general x60, matrix products, sweep(): product = jnp.einsum('mbc,mcd->mbd', system, approx, precision=high)  32.8 us
    dot_general x60, matrix products, sweep(): jnp.einsum('mbc,mcd->mbd', approx, product, precision=high)  23.8 us
    all_to_all x1, starting transfers between devices, per_device(): lax.all_to_all(meta_out.reshape(2, devices, capacity), ('dp', 'feat'), sp...  18.9 us
    psum x1, blocking collectives, per_device(): fixed_grad = lax.psum(grad_part, 'dp') / math.sqrt(rows_own * devices)  12.8 us
    all_to_all x1, waiting for transfers between devices, per_device(): lax.all_to_all(back_value.reshape(devices, capacity), ('dp', 'feat'), spl...  9.8 us
    all_to_all x1, starting transfers between devices, per_device(): lax.all_to_all(rows_out.reshape(devices, capacity, width), ('dp', 'feat')...  9.4 us
    all_to_all x1, starting transfers between devices, per_device(): lax.all_to_all(back_value.reshape(devices, capacity), ('dp', 'feat'), spl...  6.99 us
  transfers between devices with their start and end apart: 3, of which 2 were waited for; matrix products, arithmetic and copies ran while one was open for 7% of the time, Pallas kernels for 0%

commit v1 on v0

--- a/solution.py
+++ b/solution.py
@@ -63,7 +63,7 @@
     coef_half = fixed_coef.astype(jnp.bfloat16)
     partial_score = jnp.dot(features, coef_half, preferred_element_type=jnp.float32)
     own_clicks = lax.dynamic_slice_in_dim(clicks, row_start, rows_own).astype(jnp.float32)
-    fixed_score = lax.psum(partial_score, "feat")
+    fixed_score = jnp.sum(lax.all_gather(partial_score, "feat"), axis=0)
     residual = (jax.nn.sigmoid(fixed_score + member_score) - clicks.astype(jnp.float32)).astype(
         jnp.bfloat16
     )

time: 236 us -> 189 us (0.80)
  blocking collectives: 75.1 us -> 33.5 us
  starting transfers between devices: 35.3 us -> 29.3 us
    psum x1 -> x0, blocking collectives: 62.3 us -> none  [per_device(): fixed_score = lax.psum(partial_score, 'feat')]
    all_gather x0 -> x1, blocking collectives: none -> 20.7 us  [per_device(): fixed_score = jnp.sum(lax.all_gather(partial_score, 'feat'), axis=0)]
    all_to_all x1, starting transfers between devices: 18.9 us -> 12.9 us  [per_device(): lax.all_to_all(meta_out.reshape(2, devices, capacity), ('dp', 'feat'), sp...]
  transfers between devices with their start and end apart: 3 -> 3, of which waited for: 2 -> 2; matrix products, arithmetic and copies ran while one was open for 7% -> 9% of each run, Pallas kernels for 0% -> 0%
where the time goes in v1:
time: 189 us; the launch traced here: 188 us
  matrix products  70.7 us (37%)
  blocking collectives  33.5 us (18%)
  local copies, waits for them, and re-layouts  32.7 us (17%)
  starting transfers between devices  29.3 us (16%)
  waiting for transfers between devices  12.6 us (7%)
  other arithmetic  5.87 us (3%)
  loops' own time  2.3 us (1%)
    dot_general x60, matrix products, sweep(): product = jnp.einsum('mbc,mcd->mbd', system, approx, precision=high)  32.8 us
    dot_general x60, matrix products, sweep(): jnp.einsum('mbc,mcd->mbd', approx, product, precision=high)  23.8 us
    all_gather x1, blocking collectives, per_device(): fixed_score = jnp.sum(lax.all_gather(partial_score, 'feat'), axis=0)  20.7 us
    all_to_all x1, starting transfers between devices, per_device(): lax.all_to_all(meta_out.reshape(2, devices, capacity), ('dp', 'feat'), sp...  12.9 us
    psum x1, blocking collectives, per_device(): fixed_grad = lax.psum(grad_part, 'dp') / math.sqrt(rows_own * devices)  12.8 us
    all_to_all x1, waiting for transfers between devices, per_device(): lax.all_to_all(back_value.reshape(devices, capacity), ('dp', 'feat'), spl...  9.8 us
    all_to_all x1, starting transfers between devices, per_device(): lax.all_to_all(rows_out.reshape(devices, capacity, width), ('dp', 'feat')...  9.4 us
    all_to_all x1, starting transfers between devices, per_device(): lax.all_to_all(back_value.reshape(devices, capacity), ('dp', 'feat'), spl...  6.99 us
  transfers between devices with their start and end apart: 3, of which 2 were waited for; matrix products, arithmetic and copies ran while one was open for 9% of the time, Pallas kernels for 0%

profile of v1, /device:TPU:1, one launch (start us, length us, event | category | flops | bytes accessed | tf_op | source)
XLA Modules:
  0.0 188.1 jit_solution(16374158221362843522)
XLA Ops:
  0.6 0.8 convert_add_fusion
  2.0 0.7 convert_element_type.65
  2.7 3.4 %fusion.54 = f32[1,4096]{1,0:T(1,128)S(1)} fusion(bf16[4096,512]{1,0:T(8,128)(2,1)} %param.13, bf16[512,1]{0,1:T(2,128)(2,1)S(1)} %reshape.294), kind=kOutput, calls=%fused_computation.124 | convolution fusion | flops 4194304 | bytes 4211712 | tf_op jit(solution)/shard_map/dot_general | solution.py:64
  6.1 20.7 %all-gather = f32[65536]{0:T(1024)S(1)} all-gather(f32[4096]{0:T(1024)S(1)} %bitcast.212), channel_id=2, replica_groups=mesh['dp'=8,'feat'=16] {'feat'}, dimensions={0}, use_global_device_ids=true | all-gather | bytes 278528 | tf_op jit(solution)/shard_map/all_gather | solution.py:66
  27.0 1.4 scatter_custom_fusion
  28.5 1.4 scatter_custom_fusion.1
  30.1 0.8 copy.54
  30.9 12.9 %all-to-all-start = ((f32[2,128,6]{2,0,1:T(2,128)}), f32[2,128,6]{2,0,1:T(2,128)S(1)}, u32[]{:S(2)}, u32[]{:S(2)}) async-start(f32[2,128,6]{2,0,1:T(2,128)} %copy.54), calls=%async_computation | async-start | bytes 262144 | tf_op jit(solution)/shard_map/all_to_all | solution.py:92
  43.9 2.8 %fusion.55 = f32[1,512]{1,0:T(1,128)S(1)} fusion(bf16[4096,1]{0,1:T(2,128)(2,1)S(1)} %reshape.296, bf16[4096,512]{1,0:T(8,128)(2,1)} %param.13), kind=kOutput, calls=%fused_computation.125 | convolution fusion | flops 4194304 | bytes 4204544 | tf_op jit(solution)/shard_map/dot_general | solution.py:71
  46.7 12.8 %psum.7 = f32[512]{0:T(512)S(1)} all-reduce(f32[512]{0:T(512)S(1)} %bitcast.239), channel_id=1, replica_groups=mesh['dp'=8,'feat'=16] {'dp'}, use_global_device_ids=true, to_apply=%region_1.0 | all-reduce | flops 512 | bytes 4096 | tf_op jit(solution)/shard_map/psum | solution.py:72
  59.5 0.6 broadcast_multiply_fusion.3
  60.1 2.0 %scatter_custom_fusion.2 = bf16[768,256]{1,0:T(8,128)(2,1)S(1)} fusion(s32[256]{0:T(256)S(1)} %compare_select_fusion.8, bf16[256,256]{1,0:T(8,128)(2,1)} %param.17, bf16[]{:T(256)} %constant.104.clone.1), kind=kCustom, calls=%fused_computation.24 | custom fusion | bytes 393728 | tf_op jit(solution)/shard_map/scatter | solution.py:79
  62.1 0.9 reshape.209
  63.0 9.4 %all-to-all-start.1 = ((bf16[128,6,256]{2,1,0:T(8,128)(2,1)}), bf16[128,6,256]{2,1,0:T(8,128)(2,1)S(1)}, u32[]{:S(2)}, u32[]{:S(2)}) async-start(bf16[128,6,256]{2,1,0:T(8,128)(2,1)} %reshape.209), calls=%async_computation.1 | async-start | bytes 1048576 | tf_op jit(solution)/shard_map/all_to_all | solution.py:85
  73.0 3.4 %scatter_custom_fusion.6 = f32[513]{0:T(1024)S(1)} fusion(s32[768]{0:T(1024)S(1)} %get-tuple-element.94, f32[768]{0:T(1024)S(1)} %fusion.33, f32[]{:T(128)} %constant.48.clone.1), kind=kCustom, calls=%fused_computation.98 | custom fusion | bytes 2056 | tf_op jit(solution)/shard_map/scatter | solution.py:121
  76.6 3.4 %scatter_custom_fusion.5 = f32[513]{0:T(1024)S(1)} fusion(s32[768]{0:T(1024)S(1)} %get-tuple-element.94, f32[768]{0:T(1024)S(1)} %reshape.277, f32[]{:T(128)} %constant.48.clone.1), kind=kCustom, calls=%fused_computation.100 | custom fusion | bytes 2056 | tf_op jit(solution)/shard_map/scatter | solution.py:115
  80.1 3.6 %scatter_custom_fusion.4 = f32[513]{0:T(1024)S(1)} fusion(s32[768]{0:T(1024)S(1)} %get-tuple-element.94, f32[768]{0:T(1024)S(1)} %broadcast.285, f32[]{:T(128)} %constant.48.clone.1), kind=kCustom, calls=%fused_computation.102 | custom fusion | bytes 2056 | tf_op jit(solution)/shard_map/scatter | solution.py:127
  83.7 2.8 %all-to-all-done.1 = bf16[128,6,256]{2,1,0:T(8,128)(2,1)S(1)} async-done(((bf16[128,6,256]{2,1,0:T(8,128)(2,1)}), bf16[128,6,256]{2,1,0:T(8,128)(2,1)S(1)}, u32[]{:S(2)}, u32[]{:S(2)}) %all-to-all-start.1) | async-done | bytes 393248 | tf_op jit(solution)/shard_map/all_to_all | solution.py:85
  86.6 5.6 %scatter_custom_fusion.3 = f32[513,256]{1,0:T(8,128)S(1)} fusion(s32[768]{0:T(1024)S(1)} %get-tuple-element.94, f32[768,256]{1,0:T(8,128)S(1)} %reshape.261, f32[]{:T(128)} %constant.48.clone.1), kind=kCustom, calls=%fused_computation.15 | custom fusion | bytes 525316 | tf_op jit(solution)/shard_map/scatter | solution.py:109
  92.3 0.6 fusion.27
  93.9 0.6 abs_reduce_fusion.2
  94.9 20.0 %while.30 = (s32[]{:T(128)}, f32[8,64,64]{1,2,0:T(8,128)S(1)}, f32[8,64,64]{2,1,0:T(8,128)S(1)}, s32[]{:T(128)}) while((s32[]{:T(128)}, f32[8,64,64]{1,2,0:T(8,128)S(1)}, f32[8,64,64]{2,1,0:T(8,128)S(1)}, s32[]{:T(128)}) %tuple.70), condition=%wide.region_15.16_spmd, body=%wide.region_14.15_spmd.sunk | while | flops 50397184 | bytes 1048629 | solution.py:23
  116.7 0.6 fusion.21
  117.8 20.0 %while.31 = (s32[]{:T(128)}, f32[8,64,64]{1,2,0:T(8,128)S(1)}, f32[8,64,64]{2,1,0:T(8,128)S(1)}, s32[]{:T(128)}) while((s32[]{:T(128)}, f32[8,64,64]{1,2,0:T(8,128)S(1)}, f32[8,64,64]{2,1,0:T(8,128)S(1)}, s32[]{:T(128)}) %tuple.73), condition=%wide.region_19.20_spmd, body=%wide.region_18.19_spmd.sunk | while | flops 50397184 | bytes 1048629 | solution.py:23
  140.6 20.0 %while.32 = (s32[]{:T(128)}, f32[8,64,64]{1,2,0:T(8,128)S(1)}, f32[8,64,64]{2,1,0:T(8,128)S(1)}, s32[]{:T(128)}) while((s32[]{:T(128)}, f32[8,64,64]{1,2,0:T(8,128)S(1)}, f32[8,64,64]{2,1,0:T(8,128)S(1)}, s32[]{:T(128)}) %tuple.76), condition=%wide.region_23.24_spmd, body=%wide.region_22.23_spmd.sunk | while | flops 50397184 | bytes 1048629 | solution.py:23
  162.1 5.0 %gather_fusion = f32[768]{0:T(1024)S(1)} fusion(f32[512]{0:T(512)S(1)} %reshape.214, s32[1024]{0:T(1024)S(1)} %pad_clamp_fusion.1), kind=kCustom, calls=%fused_computation | custom fusion | bytes 9216 | tf_op jit(solution)/shard_map/gather | solution.py:132
  167.2 0.6 bitcast_select_fusion.1
  167.8 7.0 %all-to-all-start.2 = ((f32[128,1,6]{2,1,0:T(1,128)}), f32[128,1,6]{2,1,0:T(1,128)S(1)}, u32[]{:S(2)}, u32[]{:S(2)}) async-start(f32[128,1,6]{2,1,0:T(1,128)} %bitcast.62), calls=%async_computation.2 | async-start | bytes 131072 | tf_op jit(solution)/shard_map/all_to_all | solution.py:133
  174.9 9.8 %all-to-all-done.2 = f32[128,1,6]{2,1,0:T(1,128)S(1)} async-done(((f32[128,1,6]{2,1,0:T(1,128)}), f32[128,1,6]{2,1,0:T(1,128)S(1)}, u32[]{:S(2)}, u32[]{:S(2)}) %all-to-all-start.2) | async-done | bytes 3104 | tf_op jit(solution)/shard_map/all_to_all | solution.py:133
  185.2 0.8 reduce.11
  186.1 1.4 gather_fusion.1
  187.5 0.6 dynamic-slice_add_fusion
  (273 shorter events, 68.4 us)
Async XLA Ops:
  1.8 42.0 %copy-start.2 = (s32[4096]{0:T(1024)S(1)}, s32[4096]{0:T(1024)}, u32[]{:S(2)}) copy-start(s32[4096]{0:T(1024)} %param.16) | copy-start | bytes 49156
  1.8 42.0 %copy-start.3 = (f32[4096]{0:T(1024)S(1)}, f32[4096]{0:T(1024)}, u32[]{:S(2)}) copy-start(f32[4096]{0:T(1024)} %param.15) | copy-start | bytes 49156
  30.9 32.2 %all-to-all-start = ((f32[2,128,6]{2,0,1:T(2,128)}), f32[2,128,6]{2,0,1:T(2,128)S(1)}, u32[]{:S(2)}, u32[]{:S(2)}) async-start(f32[2,128,6]{2,0,1:T(2,128)} %copy.54), calls=%async_computation | async-start | bytes 262144 | tf_op jit(solution)/shard_map/all_to_all | solution.py:92
  43.9 48.4 %copy-start = (f32[8,256]{1,0:T(8,128)S(1)}, f32[8,256]{1,0:T(8,128)}, u32[]{:S(2)}) copy-start(f32[8,256]{1,0:T(8,128)} %param.18) | copy-start | bytes 24580
  63.0 23.5 %all-to-all-start.1 = ((bf16[128,6,256]{2,1,0:T(8,128)(2,1)}), bf16[128,6,256]{2,1,0:T(8,128)(2,1)S(1)}, u32[]{:S(2)}, u32[]{:S(2)}) async-start(bf16[128,6,256]{2,1,0:T(8,128)(2,1)} %reshape.209), calls=%async_computation.1 | async-start | bytes 1048576 | tf_op jit(solution)/shard_map/all_to_all | solution.py:85
  161.4 26.7 %copy-start.1 = (f32[8,256]{1,0:T(8,128)}, f32[8,256]{1,0:T(8,128)S(1)}, u32[]{:S(2)}) copy-start(f32[8,256]{1,0:T(8,128)S(1)} %fusion.12) | copy-start | bytes 24580
  167.8 16.8 %all-to-all-start.2 = ((f32[128,1,6]{2,1,0:T(1,128)}), f32[128,1,6]{2,1,0:T(1,128)S(1)}, u32[]{:S(2)}, u32[]{:S(2)}) async-start(f32[128,1,6]{2,1,0:T(1,128)} %bitcast.62), calls=%async_computation.2 | async-start | bytes 131072 | tf_op jit(solution)/shard_map/all_to_all | solution.py:133
